TPU v7x, 512 devices: a whole 4x8x8 slice. The times are simulated.
512 devices in a mesh: ctx: 64 (over z, y), tp: 8 (over x, core).
Axes of the slice: x: 4, y: 8, z: 8, core: 2. Of those that a mesh axis runs over, the one named last changes fastest.
Arguments:
- span_q: bfloat16 [8192, 8192], P('ctx', 'tp'), may hold values from -21 to 21
- span_kv: bfloat16 [2, 8192, 1024], P(None, 'ctx', 'tp'), may hold values from -20 to 20
- cache_kv: bfloat16 [2, 65536, 1024], P(None, 'ctx', 'tp'), may hold values from -20 to 20
- anchor_kv: bfloat16 [2, 2048, 1024], P(None, 'ctx', 'tp'), may hold values from -20 to 20
- block_len: int32 [64], P('ctx'), may hold values from 1 to 1024, 40960 in all
- queries: bfloat16 [128, 8192], P('ctx', 'tp'), may hold values from -21 to 21
- out_weight: bfloat16 [8192, 8192], P('tp', 'ctx'), may hold values from -0.0625 to 0.0625
Outputs:
- span_out: bfloat16 [8192, 8192], P('ctx', 'tp')
- answer: bfloat16 [128, 8192], P('tp', 'ctx')
Inputs may be any that keep to these rules, and one draw needn't show every extreme that they name: The new tokens of block c follow its block_len[c] valid cache rows.
All inputs are finite; a program needn't handle non-finite values.
Results may differ from a plain program's by a relative error of at most 0.0049.
Values may be sent and summed in bfloat16 or wider, within the bound.
A program may use at most 64 MiB of HBM per device.

v0:
```python
import math
import jax
import jax.numpy as jnp
from jax import lax
from jax.sharding import PartitionSpec as P

HD = 128
masked_score = -1e30


def all_heads(query_rows, key_rows, value_rows, visible):
    row_count = query_rows.shape[0]
    head_count = query_rows.shape[1] // HD
    score_scale = 1.0 / math.sqrt(HD)

    def per_head(head_index, running):
        maxima, totals, outputs = running
        q_head = lax.dynamic_slice_in_dim(query_rows, head_index * HD, HD, 1)
        scores = (
            jnp.einsum("qd,nd->qn", q_head, key_rows, preferred_element_type=jnp.float32)
            * score_scale
        )
        scores = jnp.where(visible, scores, masked_score)
        peak_score = jnp.max(scores, axis=1, keepdims=True)
        weights = jnp.exp(scores - peak_score)
        weight_sum = jnp.sum(weights, axis=1, keepdims=True)
        product = jnp.einsum(
            "qn,nd->qd",
            weights.astype(jnp.bfloat16),
            value_rows,
            preferred_element_type=jnp.float32,
        )
        maxima = lax.dynamic_update_slice_in_dim(maxima, peak_score, head_index, 1)
        totals = lax.dynamic_update_slice_in_dim(totals, weight_sum, head_index, 1)
        outputs = lax.dynamic_update_slice_in_dim(outputs, product, head_index * HD, 1)
        return (maxima, totals, outputs)

    initial = (
        jnp.zeros((row_count, head_count), jnp.float32),
        jnp.zeros((row_count, head_count), jnp.float32),
        jnp.zeros((row_count, head_count * HD), jnp.float32),
    )
    return lax.fori_loop(0, head_count, per_head, initial)


def local(span_q, span_kv, cache_kv, anchor_kv, block_len, queries, out_weight):
    cache_count = cache_kv.shape[1]
    span_count = span_kv.shape[1]
    length = block_len[0]
    local_kv = jnp.concatenate([cache_kv, span_kv], axis=1)
    anchor_all = lax.all_gather(anchor_kv, "ctx", axis=1, tiled=True)
    query_all = lax.all_gather(queries, "ctx", axis=0, tiled=True)
    anchor_count = anchor_all.shape[1]
    first_kv = jnp.concatenate([anchor_all, local_kv], axis=1)
    key_total = first_kv.shape[1]
    column = lax.broadcasted_iota(jnp.int32, (span_count, key_total), 1)
    query_pos = lax.broadcasted_iota(jnp.int32, (span_count, key_total), 0)
    in_cache = (column >= anchor_count) & (column < anchor_count + cache_count)
    in_span = column >= anchor_count + cache_count
    visible = jnp.where(
        in_cache,
        column - anchor_count < length,
        jnp.where(in_span, column - anchor_count - cache_count <= query_pos, True),
    )
    first_max, first_sum, first_values = all_heads(span_q, first_kv[0], first_kv[1], visible)
    span_out = (first_values / jnp.repeat(first_sum, HD, axis=1)).astype(jnp.bfloat16)
    own_count = anchor_kv.shape[1]
    second_kv = jnp.concatenate([anchor_kv, local_kv], axis=1)
    column_two = lax.broadcasted_iota(jnp.int32, (1, second_kv.shape[1]), 1)
    cache_two = (column_two >= own_count) & (column_two < own_count + cache_count)
    visible_two = jnp.where(cache_two, column_two - own_count < length, True)
    part_max, part_sum, part_values = all_heads(query_all, second_kv[0], second_kv[1], visible_two)
    global_max = lax.pmax(part_max, "ctx")
    rescale = jnp.exp(part_max - global_max)
    full_sum, full_values = lax.psum(
        (part_sum * rescale, part_values * jnp.repeat(rescale, HD, axis=1)), "ctx"
    )
    attended = (full_values / jnp.repeat(full_sum, HD, axis=1)).astype(jnp.bfloat16)
    partial_value = jnp.dot(attended, out_weight, preferred_element_type=jnp.float32)
    answer = lax.psum_scatter(partial_value, "tp", scatter_dimension=0, tiled=True).astype(
        jnp.bfloat16
    )
    return (span_out, answer)


def solution(mesh):
    placed = (
        P("ctx", "tp"),
        P(None, "ctx", "tp"),
        P(None, "ctx", "tp"),
        P(None, "ctx", "tp"),
        P("ctx"),
        P("ctx", "tp"),
        P("tp", "ctx"),
    )
    return jax.shard_map(
        local,
        mesh=mesh,
        in_specs=placed,
        out_specs=(P("ctx", "tp"), P("tp", "ctx")),
        check_vma=False,
    )
```

profile of v0, /device:TPU:16, one launch (start us, length us, event | category | flops | bytes accessed | tf_op | source)
XLA Modules:
  0.0 452.8 jit_solution(17501054155772972104)
XLA Ops:
  7.2 0.7 all-gather.3.cloned.1.call-update
  8.0 56.4 %all-gather = bf16[64,2,1024]{2,1,0:T(2,128)(2,1)S(1)} all-gather(bf16[1,2,1024]{2,1,0:T(2,128)(2,1)} %bitcast.53), channel_id=1, replica_groups=mesh['ctx'=64,'tp'=8] {'ctx'}, dimensions={0}, use_global_device_ids=true | all-gather | bytes 266240 | tf_op jit(solution)/shard_map/all_gather | solution.py:52
  65.2 0.7 constant_dynamic-update-slice_fusion.5
  65.9 0.6 iota_add_fusion
  66.5 27.6 %all-gather.3.cloned.1.call-done = bf16[2,2048,128]{2,1,0:T(8,128)(2,1)} async-done(((bf16[2,32,128]{2,1,0:T(8,128)(2,1)}), bf16[2,2048,128]{2,1,0:T(8,128)(2,1)}) %all-gather.3.cloned.1.call-update) | async-done | bytes 1048592 | tf_op jit(solution)/shard_map/all_gather | solution.py:51
  94.1 1.3 constant_dynamic-update-slice_fusion.2
  95.7 0.8 copy-done.1
  96.5 1.1 slice_bitcast_fusion.2
  97.6 13.0 %while.35 = (s32[]{:T(128)}, f32[128,8]{0,1:T(8,128)S(1)}, f32[128,8]{0,1:T(8,128)S(1)}, f32[128,1024]{1,0:T(8,128)S(1)}, bf16[128,1024]{1,0:T(8,128)(2,1)S(1)},...) while((s32[]{:T(128)}, f32[128,8]{0,1:T(8,128)S(1)}, ...), condition=%wide.region_7.8_spmd.clone, body=%wide.region_4.7_spmd.clone.sunk | while | flops 78662336 | bytes 2530647 | solution.py:43
  97.7 0.7 select_reduce_fusion.2
  98.3 0.4 fusion.51
  99.3 0.7 select_reduce_fusion.2
  100.0 0.4 fusion.51
  100.3 0.3 convolution_dynamic-update-slice_fusion.5
  100.9 0.7 select_reduce_fusion.2
  101.6 0.4 fusion.51
  102.0 0.3 convolution_dynamic-update-slice_fusion.5
  102.5 0.7 select_reduce_fusion.2
  103.2 0.4 fusion.51
  103.6 0.3 convolution_dynamic-update-slice_fusion.5
  104.2 0.7 select_reduce_fusion.2
  104.8 0.4 fusion.51
  105.2 0.3 convolution_dynamic-update-slice_fusion.5
  105.8 0.7 select_reduce_fusion.2
  106.5 0.4 fusion.51
  106.8 0.3 convolution_dynamic-update-slice_fusion.5
  107.4 0.7 select_reduce_fusion.2
  108.1 0.4 fusion.51
  108.4 0.3 convolution_dynamic-update-slice_fusion.5
  109.0 0.7 select_reduce_fusion.2
  109.7 0.4 fusion.51
  110.1 0.3 convolution_dynamic-update-slice_fusion.5
  110.6 137.7 %pmax.7 = f32[128,8]{0,1:T(8,128)S(1)} all-reduce(f32[128,8]{0,1:T(8,128)S(1)} %get-tuple-element.271), channel_id=1, replica_groups=mesh['ctx'=64,'tp'=8] {'ctx'}, use_global_device_ids=true, to_apply=%region_8.9 | all-reduce | flops 1024 | bytes 8192 | tf_op jit(solution)/shard_map/pmax | solution.py:73
  248.6 0.9 bitcast_multiply_fusion
  249.8 19.4 %while.34 = (s32[]{:T(128)}, f32[128,8]{0,1:T(8,128)S(1)}, f32[128,1024]{1,0:T(8,128)S(1)}, bf16[128,1024]{1,0:T(8,128)(2,1)}, bf16[3200,128]{1,0:T(8,128)(2,1)S...) while((s32[]{:T(128)}, f32[128,8]{0,1:T(8,128)S(1)}, ...), condition=%wide.region_3.4_spmd.clone, body=%wide.region_0.3_spmd.clone.sunk | while | flops 213810944 | bytes 6681151 | solution.py:43
  249.9 1.5 fusion.46
  251.4 0.5 convolution_dynamic-update-slice_fusion.4
  251.8 0.4 fusion.47
  252.3 1.5 fusion.46
  253.8 0.5 convolution_dynamic-update-slice_fusion.4
  254.3 0.4 fusion.47
  254.7 1.5 fusion.46
  256.2 0.5 convolution_dynamic-update-slice_fusion.4
  256.7 0.4 fusion.47
  257.1 1.5 fusion.46
  258.6 0.5 convolution_dynamic-update-slice_fusion.4
  259.1 0.4 fusion.47
  259.5 1.5 fusion.46
  261.1 0.5 convolution_dynamic-update-slice_fusion.4
  261.5 0.4 fusion.47
  262.0 1.5 fusion.46
  263.5 0.5 convolution_dynamic-update-slice_fusion.4
  263.9 0.4 fusion.47
  264.4 1.5 fusion.46
  265.9 0.5 convolution_dynamic-update-slice_fusion.4
  266.4 0.4 fusion.47
  266.8 1.5 fusion.46
  268.3 0.5 convolution_dynamic-update-slice_fusion.4
  268.8 0.4 fusion.47
  269.2 138.1 %psum.15 = f32[128,8]{0,1:T(8,128)S(1)} all-reduce(f32[128,8]{0,1:T(8,128)S(1)} %get-tuple-element.354), channel_id=1, replica_groups=mesh['ctx'=64,'tp'=8] {'ctx'}, use_global_device_ids=true, to_apply=%region_10.11 | all-reduce | flops 1024 | bytes 8192 | tf_op jit(solution)/shard_map/psum | solution.py:75
  407.7 1.9 fusion.22
  409.8 0.8 fusion.21
  410.6 34.3 %reduce-scatter.2.cloned.1.call-done = f32[16,128]{1,0:T(8,128)} async-done(((f32[128,128]{1,0:T(8,128)}), f32[16,128]{1,0:T(8,128)}) %reduce-scatter.2.cloned.1.call-update) | async-done | bytes 8208 | tf_op jit(solution)/shard_map/reduce_scatter | solution.py:80
  444.9 1.3 convert_element_type.25
  (64 shorter events, 4.1 us)
Async XLA Ops:
  7.2 400.5 %copy-start = (bf16[1024,128]{1,0:T(8,128)(2,1)S(1)}, bf16[1024,128]{1,0:T(8,128)(2,1)}, u32[]{:S(2)}) copy-start(bf16[1024,128]{1,0:T(8,128)(2,1)} %param.17) | copy-start | bytes 786436
  7.2 88.2 %copy-start.2 = (bf16[2,1024,128]{2,1,0:T(8,128)(2,1)S(1)}, bf16[2,1024,128]{2,1,0:T(8,128)(2,1)}, u32[]{:S(2)}) copy-start(bf16[2,1024,128]{2,1,0:T(8,128)(2,1)} %param.13) | copy-start | bytes 1572868
  7.2 86.9 %all-gather.3.cloned.1.call-start = ((), (), s32[]{:S(2)}) async-start(), calls=%async_computation.1 | async-start | bytes 1064960 | tf_op jit(solution)/shard_map/all_gather | solution.py:51
  7.9 399.6 %all-reduce.2.cloned.1.call-start = ((), (), s32[]{:S(2)}) async-start(), calls=%async_computation.2 | async-start | bytes 1048576 | tf_op jit(solution)/shard_map/psum | solution.py:75
  66.5 29.1 %copy-start.3 = (bf16[2,128,128]{2,1,0:T(8,128)(2,1)S(1)}, bf16[2,128,128]{2,1,0:T(8,128)(2,1)}, u32[]{:S(2)}) copy-start(bf16[2,128,128]{2,1,0:T(8,128)(2,1)} %param.12) | copy-start | bytes 196612
  95.7 0.8 copy-start.1
  249.6 195.3 %reduce-scatter.2.cloned.1.call-start = ((), (), s32[]{:S(2)}) async-start(), calls=%async_computation.3 | async-start | bytes 73728 | tf_op jit(solution)/shard_map/reduce_scatter | solution.py:80
Sparse Core Ops, SparseCore 0:
  11.0 83.0 all-gather.2
  249.7 155.1 all-reduce.1
  409.7 35.1 reduce-scatter.1
where the time goes:
time: 454 us; the launch traced here: 453 us
  blocking collectives  332 us (73%)
  waiting for transfers between devices  62.6 us (14%)
  matrix products  23.1 us (5%)
  between operations  14.6 us (3%)
  other arithmetic  13.6 us (3%)
  local copies, waits for them, and re-layouts  6.12 us (1%)
    psum x1, blocking collectives, local(): lax.psum((part_sum * rescale, part_values * jnp.repeat(rescale, HD, axis=...  138 us
    pmax x1, blocking collectives, local(): global_max = lax.pmax(part_max, 'ctx')  138 us
    all_gather x1, blocking collectives, local(): query_all = lax.all_gather(queries, 'ctx', axis=0, tiled=True)  56.4 us
    reduce_scatter x1, waiting for transfers between devices, local(): lax.psum_scatter(partial_value, 'tp', scatter_dimension=0, tiled=True)  34.3 us
    all_gather x1, waiting for transfers between devices, local(): anchor_all = lax.all_gather(anchor_kv, 'ctx', axis=1, tiled=True)  27.6 us
    dot_general x16, matrix products, per_head(): jnp.einsum('qd,nd->qn', q_head, key_rows, preferred_element_type=jnp.floa...  15.1 us
  transfers between devices with their start and end apart: 3, of which 2 were waited for; matrix products, arithmetic and copies ran while one was open for 5% of the time, Pallas kernels for 0%

commit v1 on v0

--- a/solution.py
+++ b/solution.py
@@ -48,7 +48,19 @@
     span_count = span_kv.shape[1]
     length = block_len[0]
     local_kv = jnp.concatenate([cache_kv, span_kv], axis=1)
-    anchor_all = lax.all_gather(anchor_kv, "ctx", axis=1, tiled=True)
+
+    def _replace_roots(arr):
+        r2, step_out = (lax.axis_size("ctx"), lax.axis_index("ctx"))
+        even, last = (arr, 1)
+        while last < r2:
+            x_now = lax.ppermute(even, "ctx", list(map(lambda j0: (j0, j0 ^ last), range(r2))))
+            v_now = jnp.concatenate([even, x_now], axis=1)
+            clean = jnp.concatenate([x_now, even], axis=1)
+            even = jnp.where(step_out & last == 0, v_now, clean)
+            last = 2 * last
+        return even
+
+    anchor_all = _replace_roots(anchor_kv)
     query_all = lax.all_gather(queries, "ctx", axis=0, tiled=True)
     anchor_count = anchor_all.shape[1]
     first_kv = jnp.concatenate([anchor_all, local_kv], axis=1)

time: 454 us -> 463 us (1.020)
  the two profiles are of different devices: /device:TPU:16 before, /device:TPU:8 now
where the time goes in v1:
time: 463 us; the launch traced here: 462 us
  blocking collectives  331 us (71%)
  waiting for transfers between devices  53.2 us (11%)
  matrix products  22.9 us (5%)
  starting transfers between devices  20.5 us (4%)
  between operations  15 us (3%)
  other arithmetic  13.7 us (3%)
  local copies, waits for them, and re-layouts  4.7 us (1%)
    psum x1, blocking collectives, local(): lax.psum((part_sum * rescale, part_values * jnp.repeat(rescale, HD, axis=...  140 us
    pmax x1, blocking collectives, local(): global_max = lax.pmax(part_max, 'ctx')  139 us
    all_gather x1, blocking collectives, local(): query_all = lax.all_gather(queries, 'ctx', axis=0, tiled=True)  51.6 us
    reduce_scatter x1, waiting for transfers between devices, local(): lax.psum_scatter(partial_value, 'tp', scatter_dimension=0, tiled=True)  31.9 us
    ppermute x6, waiting for transfers between devices, _replace_roots(): lax.ppermute(even, 'ctx', list(map(lambda j0: (j0, j0 ^ last), range(r2))))  21.3 us
    ppermute x6, starting transfers between devices, _replace_roots(): lax.ppermute(even, 'ctx', list(map(lambda j0: (j0, j0 ^ last), range(r2))))  20.4 us
    dot_general x16, matrix products, per_head(): jnp.einsum('qd,nd->qn', q_head, key_rows, preferred_element_type=jnp.floa...  15 us
  transfers between devices with their start and end apart: 8, of which 4 were waited for; matrix products, arithmetic and copies ran while one was open for 4% of the time, Pallas kernels for 0%

profile of v1, /device:TPU:8, one launch (start us, length us, event | category | flops | bytes accessed | tf_op | source)
XLA Modules:
  0.0 461.9 jit_solution(14460880291155599596)
XLA Ops:
  7.2 7.8 %collective-permute-start = (bf16[2,32,128]{2,1,0:T(8,128)(2,1)}, bf16[2,32,128]{2,1,0:T(8,128)(2,1)S(1)}, u32[]{:S(2)}, u32[]{:S(2)}) collective-permute-start(bf16[2,32,128]{2,1,0:T(8,128)(2,1)} %param.14), channel_id=1, source_target_pairs={{0,8},{8,0},{16,24},{24,16},{32,40},{40,32},{48,56},{56,48},{64,72... | collective-permute-start | bytes 49160 | tf_op jit(solution)/shard_map/ppermute | solution.py:56
  15.1 0.7 constant_dynamic-update-slice_fusion.2
  15.8 1.1 constant_dynamic-update-slice_fusion.1
  16.9 0.9 constant_dynamic-update-slice_fusion
  17.8 51.6 %all-gather = bf16[64,2,1024]{2,1,0:T(2,128)(2,1)S(1)} all-gather(bf16[1,2,1024]{2,1,0:T(2,128)(2,1)S(1)} %bitcast.53), channel_id=1, replica_groups=mesh['ctx'=64,'tp'=8] {'ctx'}, dimensions={0}, use_global_device_ids=true | all-gather | bytes 266240 | tf_op jit(solution)/shard_map/all_gather | solution.py:64
  69.6 4.0 collective-permute-start.1
  73.6 13.0 %while.35 = (s32[]{:T(128)}, f32[128,8]{0,1:T(8,128)S(1)}, f32[128,8]{0,1:T(8,128)S(1)}, f32[128,1024]{1,0:T(8,128)S(1)}, bf16[128,1024]{1,0:T(8,128)(2,1)S(1)},...) while((s32[]{:T(128)}, f32[128,8]{0,1:T(8,128)S(1)}, ...), condition=%wide.region_7.8_spmd.clone, body=%wide.region_4.7_spmd.clone.sunk | while | flops 78662336 | bytes 2530647 | solution.py:43
  73.7 0.7 select_reduce_fusion.2
  74.3 0.4 fusion.51
  75.3 0.7 select_reduce_fusion.2
  76.0 0.4 fusion.51
  76.9 0.7 select_reduce_fusion.2
  77.6 0.4 fusion.51
  77.9 0.3 convolution_dynamic-update-slice_fusion.5
  78.5 0.7 select_reduce_fusion.2
  79.2 0.4 fusion.51
  79.6 0.3 convolution_dynamic-update-slice_fusion.5
  80.1 0.7 select_reduce_fusion.2
  80.8 0.4 fusion.51
  81.8 0.7 select_reduce_fusion.2
  82.4 0.4 fusion.51
  83.4 0.7 select_reduce_fusion.2
  84.1 0.4 fusion.51
  85.0 0.7 select_reduce_fusion.2
  85.7 0.4 fusion.51
  86.6 139.2 %pmax.7 = f32[128,8]{0,1:T(8,128)S(1)} all-reduce(f32[128,8]{0,1:T(8,128)S(1)} %get-tuple-element.271), channel_id=1, replica_groups=mesh['ctx'=64,'tp'=8] {'ctx'}, use_global_device_ids=true, to_apply=%region_8.9 | all-reduce | flops 1024 | bytes 8192 | tf_op jit(solution)/shard_map/pmax | solution.py:85
  225.9 1.9 collective-permute-start.2
  227.9 8.1 %collective-permute-done.2 = bf16[2,128,128]{2,1,0:T(8,128)(2,1)S(1)} collective-permute-done((bf16[2,128,128]{2,1,0:T(8,128)(2,1)S(1)}, bf16[2,128,128]{2,1,0:T(8,128)(2,1)S(1)}, u32[]{:S(2)}, u32[]{:S(2)}) %collective-permute-start.2) | collective-permute-done | bytes 65568 | tf_op jit(solution)/shard_map/ppermute | solution.py:56
  236.0 1.9 collective-permute-start.3
  238.2 0.9 bitcast_multiply_fusion
  239.2 3.7 collective-permute-done.3
  243.0 1.9 collective-permute-start.4
  245.6 9.5 %collective-permute-done.4 = bf16[2,512,128]{2,1,0:T(8,128)(2,1)S(1)} collective-permute-done((bf16[2,512,128]{2,1,0:T(8,128)(2,1)S(1)}, bf16[2,512,128]{2,1,0:T(8,128)(2,1)S(1)}, u32[]{:S(2)}, u32[]{:S(2)}) %collective-permute-start.4) | collective-permute-done | bytes 262176 | tf_op jit(solution)/shard_map/ppermute | solution.py:56
  255.3 2.9 collective-permute-start.5
  258.2 140.4 %psum.15 = f32[128,8]{0,1:T(8,128)S(1)} all-reduce(f32[128,8]{0,1:T(8,128)S(1)} %get-tuple-element.354), channel_id=1, replica_groups=mesh['ctx'=64,'tp'=8] {'ctx'}, use_global_device_ids=true, to_apply=%region_10.11 | all-reduce | flops 1024 | bytes 8192 | tf_op jit(solution)/shard_map/psum | solution.py:87
  399.0 1.9 fusion.22
  400.9 31.9 %reduce-scatter.2.cloned.1.call-done = f32[16,128]{1,0:T(8,128)} async-done(((f32[128,128]{1,0:T(8,128)}), f32[16,128]{1,0:T(8,128)}) %reduce-scatter.2.cloned.1.call-update) | async-done | bytes 8208 | tf_op jit(solution)/shard_map/reduce_scatter | solution.py:92
  432.8 1.3 convert_element_type.25
  434.7 19.2 %while.34 = (s32[]{:T(128)}, f32[128,8]{0,1:T(8,128)S(1)}, f32[128,1024]{1,0:T(8,128)S(1)}, bf16[128,1024]{1,0:T(8,128)(2,1)}, bf16[3200,128]{1,0:T(8,128)(2,1)S...) while((s32[]{:T(128)}, f32[128,8]{0,1:T(8,128)S(1)}, ...), condition=%wide.region_3.4_spmd.clone, body=%wide.region_0.3_spmd.clone.sunk | while | flops 213810944 | bytes 6677567 | solution.py:43
  434.7 1.5 fusion.46
  436.2 0.4 convolution_dynamic-update-slice_fusion.4
  436.7 0.4 fusion.47
  437.1 1.5 fusion.46
  438.6 0.4 convolution_dynamic-update-slice_fusion.4
  439.1 0.4 fusion.47
  439.5 1.5 fusion.46
  441.0 0.4 convolution_dynamic-update-slice_fusion.4
  441.5 0.4 fusion.47
  441.9 1.5 fusion.46
  443.4 0.4 convolution_dynamic-update-slice_fusion.4
  443.9 0.4 fusion.47
  444.3 1.5 fusion.46
  445.8 0.4 convolution_dynamic-update-slice_fusion.4
  446.3 0.4 fusion.47
  446.7 1.5 fusion.46
  448.2 0.4 convolution_dynamic-update-slice_fusion.4
  448.7 0.4 fusion.47
  449.1 1.5 fusion.46
  450.6 0.4 convolution_dynamic-update-slice_fusion.4
  451.1 0.4 fusion.47
  451.5 1.5 fusion.46
  453.0 0.4 convolution_dynamic-update-slice_fusion.4
  453.5 0.4 fusion.47
  454.2 0.8 fusion.21
  (81 shorter events, 6.1 us)
Async XLA Ops:
  7.2 391.8 %copy-start = (bf16[1024,128]{1,0:T(8,128)(2,1)S(1)}, bf16[1024,128]{1,0:T(8,128)(2,1)}, u32[]{:S(2)}) copy-start(bf16[1024,128]{1,0:T(8,128)(2,1)} %param.17) | copy-start | bytes 786436
  7.2 62.4 %copy-start.3 = (bf16[2,32,128]{2,1,0:T(8,128)(2,1)S(1)}, bf16[2,32,128]{2,1,0:T(8,128)(2,1)}, u32[]{:S(2)}) copy-start(bf16[2,32,128]{2,1,0:T(8,128)(2,1)} %param.14) | copy-start | bytes 49156
  7.2 10.6 %copy-start.4 = (bf16[2,1024]{1,0:T(2,128)(2,1)S(1)}, bf16[2,1024]{1,0:T(2,128)(2,1)}, u32[]{:S(2)}) copy-start(bf16[2,1024]{1,0:T(2,128)(2,1)} %param.16) | copy-start | bytes 12292
  7.2 391.5 %all-reduce.2.cloned.1.call-start = ((), (), s32[]{:S(2)}) async-start(), calls=%async_computation.1 | async-start | bytes 1048576 | tf_op jit(solution)/shard_map/psum | solution.py:87
  7.2 62.3 %collective-permute-start = (bf16[2,32,128]{2,1,0:T(8,128)(2,1)}, bf16[2,32,128]{2,1,0:T(8,128)(2,1)S(1)}, u32[]{:S(2)}, u32[]{:S(2)}) collective-permute-start(bf16[2,32,128]{2,1,0:T(8,128)(2,1)} %param.14), channel_id=1, source_target_pairs={{0,8},{8,0},{16,24},{24,16},{32,40},{40,32},{48,56},{56,48},{64,72... | collective-permute-start | bytes 49160 | tf_op jit(solution)/shard_map/ppermute | solution.py:56
  69.6 156.3 %collective-permute-start.1 = (bf16[2,64,128]{2,1,0:T(8,128)(2,1)S(1)}, bf16[2,64,128]{2,1,0:T(8,128)(2,1)S(1)}, u32[]{:S(2)}, u32[]{:S(2)}) collective-permute-start(bf16[2,64,128]{2,1,0:T(8,128)(2,1)S(1)} %maximum_select_fusion.5), channel_id=1, source_target_pairs={{0,16},{8,24},{16,0},{24,8},{32,48},{40,56},{48,32},{56,40},{64,80... | collective-permute-start | bytes 98312 | tf_op jit(solution)/shard_map/ppermute | solution.py:56
  225.9 10.1 %collective-permute-start.2 = (bf16[2,128,128]{2,1,0:T(8,128)(2,1)S(1)}, bf16[2,128,128]{2,1,0:T(8,128)(2,1)S(1)}, u32[]{:S(2)}, u32[]{:S(2)}) collective-permute-start(bf16[2,128,128]{2,1,0:T(8,128)(2,1)S(1)} %maximum_select_fusion.4), channel_id=1, source_target_pairs={{0,32},{8,40},{16,48},{24,56},{32,0},{40,8},{48,16},{56,24},{64,96... | collective-permute-start | bytes 196616 | tf_op jit(solution)/shard_map/ppermute | solution.py:56
  236.0 6.9 %collective-permute-start.3 = (bf16[2,256,128]{2,1,0:T(8,128)(2,1)S(1)}, bf16[2,256,128]{2,1,0:T(8,128)(2,1)S(1)}, u32[]{:S(2)}, u32[]{:S(2)}) collective-permute-start(bf16[2,256,128]{2,1,0:T(8,128)(2,1)S(1)} %maximum_select_fusion.3), channel_id=1, source_target_pairs={{0,64},{8,72},{16,80},{24,88},{32,96},{40,104},{48,112},{56,120},{... | collective-permute-start | bytes 393224 | tf_op jit(solution)/shard_map/ppermute | solution.py:56
  239.1 193.6 %reduce-scatter.2.cloned.1.call-start = ((), (), s32[]{:S(2)}) async-start(), calls=%async_computation.2 | async-start | bytes 73728 | tf_op jit(solution)/shard_map/reduce_scatter | solution.py:92
  243.0 12.1 %collective-permute-start.4 = (bf16[2,512,128]{2,1,0:T(8,128)(2,1)S(1)}, bf16[2,512,128]{2,1,0:T(8,128)(2,1)S(1)}, u32[]{:S(2)}, u32[]{:S(2)}) collective-permute-start(bf16[2,512,128]{2,1,0:T(8,128)(2,1)S(1)} %maximum_select_fusion.2), channel_id=1, source_target_pairs={{0,128},{8,136},{16,144},{24,152},{32,160},{40,168},{48,176},{56,1... | collective-permute-start | bytes 786440 | tf_op jit(solution)/shard_map/ppermute | solution.py:56
  255.3 178.8 %collective-permute-start.5 = (bf16[2,1024,128]{2,1,0:T(8,128)(2,1)S(1)}, bf16[2,1024,128]{2,1,0:T(8,128)(2,1)S(1)}, u32[]{:S(2)}, u32[]{:S(2)}) collective-permute-start(bf16[2,1024,128]{2,1,0:T(8,128)(2,1)S(1)} %maximum_select_fusion.1), channel_id=1, source_target_pairs={{0,256},{8,264},{16,272},{24,280},{32,288},{40,296},{48,304},{56,3... | collective-permute-start | bytes 1572872 | tf_op jit(solution)/shard_map/ppermute | solution.py:56
  400.9 33.5 %copy-start.1 = (bf16[2,1024,128]{2,1,0:T(8,128)(2,1)S(1)}, bf16[2,1024,128]{2,1,0:T(8,128)(2,1)}, u32[]{:S(2)}) copy-start(bf16[2,1024,128]{2,1,0:T(8,128)(2,1)} %param.13) | copy-start | bytes 1572868
  400.9 33.5 %copy-start.2 = (bf16[2,128,128]{2,1,0:T(8,128)(2,1)S(1)}, bf16[2,128,128]{2,1,0:T(8,128)(2,1)}, u32[]{:S(2)}) copy-start(bf16[2,128,128]{2,1,0:T(8,128)(2,1)} %param.12) | copy-start | bytes 196612
Sparse Core Ops, SparseCore 0:
  239.3 156.0 all-reduce.1
  401.0 31.7 reduce-scatter.1
